TPU v7x, 32 devices: a whole 2x2x4 slice. The times are simulated.
32 devices in a mesh: groups: 2 (over y), mem: 8 (over z, x), lat: 2 (over core).
Axes of the slice: x: 2, y: 2, z: 4, core: 2. Of those that a mesh axis runs over, the one named last changes fastest.
Arguments:
- ensemble: float32 [16, 6, 256, 512], P(('groups', 'mem'), None, 'lat'), parts along dimension 0, may hold values from -1.5 to 1.5
- forcing_table: float32 [8, 256, 512], P(None, 'lat'), may hold values from -3 to 3
- ancestors: int32 [16], P('groups'), parts along dimension 0, may hold values from 0 to 7
- selector: int32 [16], P(('groups', 'mem')), parts along dimension 0, may hold values from 0 to 7
Outputs:
- advanced: float32 [16, 6, 256, 512], P(('groups', 'mem'), None, 'lat'), parts along dimension 0
There are 2 independent parts, one for each index of `groups`. A program takes and returns all parts, laid end to end along the dimension named above; an argument that names none is the same for every part. Nothing has to cross between parts.
Inputs may be any that keep to these rules, and one draw needn't show every extreme that they name: `ancestors`: index of a member of the same ensemble; some parents are named by several slots, many by none. `selector`: index of a forcing pattern.
All inputs are finite; a program needn't handle non-finite values.
Results may differ from a plain program's by a relative error of at most 0.00002.
Values sent between devices are 32-bit elements; how exact they have to be, the bound alone decides.
No kernel may reach another device: no remote copies, remote signals or barrier semaphores. Data moves between devices by JAX's collectives and lax.ppermute only.
A program may use at most 192 MiB of HBM per device.

v0:
```python
import jax
import jax.numpy as jnp
from jax import lax
from jax.sharding import PartitionSpec as P

STEPS = 3


TIME_STEP = 0.25
DENSITY_RATIO = 0.9
DRAG_RATE = 0.1
CORIOLIS_MEAN = 0.5


def padded(block, sides, width):
    for axis, dim in sides:
        count = lax.axis_size(axis)
        forward = [(i, i + 1) for i in range(count - 1)]
        backward = [(target, source) for source, target in forward]
        low = lax.ppermute(
            lax.slice_in_dim(block, block.shape[dim] - width, None, axis=dim), axis, forward
        )
        high = lax.ppermute(lax.slice_in_dim(block, 0, width, axis=dim), axis, backward)
        block = jnp.concatenate([low, block, high], axis=dim)
    return block


def row_below(values):
    widths = [(0, 0)] * (values.ndim - 2) + [(1, 0), (0, 0)]
    return jnp.pad(values[..., :-1, :], widths)


def row_above(values):
    widths = [(0, 0)] * (values.ndim - 2) + [(0, 1), (0, 0)]
    return jnp.pad(values[..., 1:, :], widths)


def col_west(values):
    return jnp.roll(values, 1, axis=-1)


def col_east(values):
    return jnp.roll(values, -1, axis=-1)


def advance(fields, forcing, row_ids, total):
    inside = ((row_ids >= 0.0) & (row_ids < total)).astype(jnp.float32)[:, None]
    wall_mask = ((row_ids >= 1.0) & (row_ids < total)).astype(jnp.float32)[:, None]
    coriolis_u = CORIOLIS_MEAN + (row_ids / total - 0.5)[:, None]
    coriolis_v = CORIOLIS_MEAN + ((row_ids - 0.5) / total - 0.5)[:, None]
    heights = []
    zonal = []
    merid = []
    for layer_index in range(2):
        height = fields[:, 3 * layer_index]
        speed_u = fields[:, 3 * layer_index + 1]
        speed_v = fields[:, 3 * layer_index + 2] * wall_mask
        thickness = 1.0 + height
        flux_x = speed_u * (0.5 * (thickness + col_west(thickness)))
        flux_y = speed_v * (0.5 * (thickness + row_below(thickness)))
        divergence = col_east(flux_x) - flux_x + (row_above(flux_y) - flux_y)
        heights.append(height - TIME_STEP * divergence)
        zonal.append(speed_u)
        merid.append(speed_v)
    pressures = [heights[0] + heights[1], DENSITY_RATIO * heights[0] + heights[1]]
    outputs = []
    for layer_index in range(2):
        speed_u = zonal[layer_index]
        speed_v = merid[layer_index]
        pressure = pressures[layer_index]
        extra = forcing if layer_index == 0 else -DRAG_RATE * speed_u
        above_v = row_above(speed_v)
        mean_v = 0.25 * (speed_v + col_west(speed_v) + above_v + col_west(above_v))
        new_u = speed_u + TIME_STEP * (
            coriolis_u * mean_v - (pressure - col_west(pressure)) + extra
        )
        below_u = row_below(speed_u)
        mean_u = 0.25 * (speed_u + col_east(speed_u) + below_u + col_east(below_u))
        new_v = (
            speed_v + TIME_STEP * (-coriolis_v * mean_u - (pressure - row_below(pressure)))
        ) * wall_mask
        outputs.extend([heights[layer_index] * inside, new_u * inside, new_v * inside])
    return jnp.stack(outputs, axis=1)


def copy_members(block, ancestors):
    slots, fields_count, band_rows, columns = block.shape
    flat = block.reshape(slots, fields_count, band_rows * columns)
    taken = jnp.take(
        lax.all_to_all(flat, "mem", split_axis=2, concat_axis=0, tiled=True), ancestors, axis=0
    )
    moved = lax.all_to_all(taken, "mem", split_axis=0, concat_axis=2, tiled=True)
    return moved.reshape(slots, fields_count, band_rows, columns)


def pick_forcing(table, selector):
    patterns = jnp.arange(table.shape[0], dtype=jnp.int32)
    chosen = selector[:, None, None, None] == patterns[None, :, None, None]
    return jnp.sum(jnp.where(chosen, table[None], jnp.float32(0.0)), axis=1)


def on_device(ensemble, forcing_table, ancestors, selector):
    slots, fields_count, band_rows, columns = ensemble.shape
    total = jnp.float32(band_rows * lax.axis_size("lat"))
    base_row = (lax.axis_index("lat") * band_rows).astype(jnp.float32)
    margin = 2 * STEPS
    parents = copy_members(ensemble, ancestors)
    slot_forcing = pick_forcing(forcing_table, selector)
    row_ids = base_row - margin + jnp.arange(band_rows + 2 * margin).astype(jnp.float32)
    combined = jnp.concatenate([parents, slot_forcing[:, None]], axis=1)
    extended = padded(combined, (("lat", 2),), margin)
    fields = extended[:, :fields_count]
    wide_forcing = extended[:, fields_count]
    for step_index in range(STEPS):
        fields = advance(fields, wide_forcing, row_ids, total)
    return fields[:, :, margin:-margin]


def solution(mesh):
    placed = (
        P(("groups", "mem"), None, "lat", None),
        P(None, "lat", None),
        P("groups"),
        P(("groups", "mem")),
    )
    return jax.shard_map(
        on_device,
        mesh=mesh,
        in_specs=placed,
        out_specs=P(("groups", "mem"), None, "lat", None),
        check_vma=False,
    )
```

profile of v0, /device:TPU:0, one launch (start us, length us, event | category | flops | bytes accessed | tf_op | source)
XLA Modules:
  0.0 556.4 jit_solution(10381373765545520294)
XLA Ops:
  0.0 17.9 %copy.16 = f32[1,6,128,512]{1,3,2,0:T(8,128)} copy(f32[1,6,128,512]{3,2,1,0:T(8,128)} %param.4) | data formatting | bytes 3145728 | tf_op jit(solution)/shard_map/reshape | solution.py:88
  17.9 0.6 broadcast.413
  18.5 291.0 %reduce.2 = f32[65536,6]{1,0:T(8,128)} reduce(f32[65536,1,6]{2,1,0:T(1,128)} %bitcast.133, f32[]{:T(128)} %broadcast.413), dimensions={1}, to_apply=%bitcast.84.reduce_sub_computation | reduce | bytes 3145732
  309.4 33.8 %reshape.545 = f32[8,1,49152]{2,1,0:T(1,128)} reshape(f32[65536,6]{1,0:T(8,128)} %reduce.2) | data formatting | bytes 3145728
  343.3 7.6 %all-to-all-start = ((f32[8,1,49152]{2,1,0:T(1,128)}), f32[8,1,49152]{2,1,0:T(1,128)S(1)}, u32[]{:S(2)}, u32[]{:S(2)}) async-start(f32[8,1,49152]{2,1,0:T(1,128)} %reshape.545), calls=%async_computation | async-start | bytes 3145728 | tf_op jit(solution)/shard_map/all_to_all | solution.py:90
  350.9 36.8 %all-to-all-done = f32[8,1,49152]{2,1,0:T(1,128)S(1)} async-done(((f32[8,1,49152]{2,1,0:T(1,128)}), f32[8,1,49152]{2,1,0:T(1,128)S(1)}, u32[]{:S(2)}, u32[]{:S(2)}) %all-to-all-start) | async-done | bytes 1572896 | tf_op jit(solution)/shard_map/all_to_all | solution.py:90
  387.7 4.4 reduce.3
  392.0 66.7 %reshape.546 = f32[65536,1,6]{2,1,0:T(1,128)} reshape(f32[8,49152]{1,0:T(8,128)S(1)} %reduce.3) | data formatting | bytes 3145728
  458.8 18.4 %copy.14 = f32[1,6,8,8192]{3,1,2,0:T(8,128)S(1)} copy(f32[1,6,8,8192]{1,3,2,0:T(8,128)} %bitcast.134) | data formatting | bytes 3145728 | tf_op jit(solution)/shard_map/all_to_all | solution.py:90
  477.2 2.0 gather_fusion
  479.2 3.2 broadcast_select_fusion
  482.4 3.6 all-to-all-start.1
  486.7 1.9 select_reduce_fusion
  488.6 45.8 %all-to-all-done.1 = f32[8,6,8192]{2,1,0:T(8,128)S(1)} async-done(((f32[8,6,8192]{2,1,0:T(8,128)}), f32[8,6,8192]{2,1,0:T(8,128)S(1)}, u32[]{:S(2)}, u32[]{:S(2)}) %all-to-all-start.1) | async-done | bytes 1572896 | tf_op jit(solution)/shard_map/all_to_all | solution.py:92
  534.4 2.1 copy.15
  536.5 1.6 reshape.535
  538.1 1.3 collective-permute-start
  539.4 1.3 collective-permute-start.1
  540.7 1.9 collective-permute-done.1
  544.7 0.5 fusion.51
  546.7 0.5 fusion.21
  548.8 0.4 fusion.160
  549.4 0.5 fusion.65
  554.6 1.3 slice.606
  (109 shorter events, 9.7 us)
Async XLA Ops:
  343.3 7.6 %copy-start = (s32[8]{0:T(128)S(1)}, s32[8]{0:T(128)}, u32[]{:S(2)}) copy-start(s32[8]{0:T(128)} %param.6) | copy-start | bytes 100
  343.3 44.4 %all-to-all-start = ((f32[8,1,49152]{2,1,0:T(1,128)}), f32[8,1,49152]{2,1,0:T(1,128)S(1)}, u32[]{:S(2)}, u32[]{:S(2)}) async-start(f32[8,1,49152]{2,1,0:T(1,128)} %reshape.545), calls=%async_computation | async-start | bytes 3145728 | tf_op jit(solution)/shard_map/all_to_all | solution.py:90
  482.4 52.1 %all-to-all-start.1 = ((f32[8,6,8192]{2,1,0:T(8,128)}), f32[8,6,8192]{2,1,0:T(8,128)S(1)}, u32[]{:S(2)}, u32[]{:S(2)}) async-start(f32[8,6,8192]{2,1,0:T(8,128)} %broadcast_select_fusion), calls=%async_computation.1 | async-start | bytes 4194304 | tf_op jit(solution)/shard_map/all_to_all | solution.py:92
  538.1 2.6 collective-permute-start
  539.4 3.2 collective-permute-start.1
where the time goes:
time: 565 us; the launch traced here: 556 us
  other arithmetic  307 us (54%)
  local copies, waits for them, and re-layouts  150 us (27%)
  waiting for transfers between devices  84.5 us (15%)
  starting transfers between devices  13.8 us (2%)
    unnamed x6, other arithmetic  292 us
    unnamed x5, local copies, waits for them, and re-layouts  101 us
    all_to_all x1, waiting for transfers between devices, copy_members(): lax.all_to_all(taken, 'mem', split_axis=0, concat_axis=2, tiled=True)  45.8 us
    all_to_all x1, waiting for transfers between devices, copy_members(): lax.all_to_all(flat, 'mem', split_axis=2, concat_axis=0, tiled=True)  36.8 us
    all_to_all x1, local copies, waits for them, and re-layouts, copy_members(): lax.all_to_all(flat, 'mem', split_axis=2, concat_axis=0, tiled=True)  18.4 us
    reshape x1, local copies, waits for them, and re-layouts, copy_members(): flat = block.reshape(slots, fields_count, band_rows * columns)  17.9 us
  transfers between devices with their start and end apart: 4, of which 3 were waited for; matrix products, arithmetic and copies ran while one was open for 0% of the time, Pallas kernels for 0%

commit v1 on v0

v1 whole, which is shorter than its diff:
```python
import functools

import jax
import jax.numpy as jnp
from jax import lax
from jax.experimental import pallas as pl
from jax.experimental.pallas import tpu as pltpu
from jax.sharding import PartitionSpec as P

STEPS = 3


TIME_STEP = 0.25
DENSITY_RATIO = 0.9
DRAG_RATE = 0.1
CORIOLIS_MEAN = 0.5

TILE = 8


def copy_members(block, ancestors):
    slots, fields_count, band_rows, columns = block.shape
    count = lax.axis_size("mem")
    pieces = block.reshape(count, slots * fields_count * band_rows // count, columns)
    spread = lax.all_to_all(pieces, "mem", split_axis=0, concat_axis=0, tiled=True)
    taken = jnp.take(spread, ancestors, axis=0, mode="clip")
    moved = lax.all_to_all(taken, "mem", split_axis=0, concat_axis=0, tiled=True)
    return moved.reshape(slots * fields_count, band_rows, columns)


def edge_rows(block):
    rows = block.shape[-2]
    dim = block.ndim - 2
    count = lax.axis_size("lat")
    place = lax.axis_index("lat")
    if count == 2:
        sent = lax.dynamic_slice_in_dim(block, (1 - place) * (rows - TILE), TILE, axis=dim)
        got = lax.ppermute(sent, "lat", [(0, 1), (1, 0)])
        return jnp.where(place > 0, got, 0.0), jnp.where(place < 1, got, 0.0)
    forward = [(i, i + 1) for i in range(count - 1)]
    backward = [(target, source) for source, target in forward]
    below = lax.ppermute(lax.slice_in_dim(block, rows - TILE, rows, axis=dim), "lat", forward)
    above = lax.ppermute(lax.slice_in_dim(block, 0, TILE, axis=dim), "lat", backward)
    return below, above


def stencil_kernel(count, place_ref, parent_ref, low_ref, high_ref, force_ref, force_low_ref, force_high_ref, out_ref, first, second, force):
    rows, columns = parent_ref.shape[1:]
    blocks = rows // TILE
    place = place_ref[0]
    total = float(rows * count)
    tile = (TILE, columns)
    sub = lax.broadcasted_iota(jnp.int32, tile, 0)
    top = sub == TILE - 1
    bottom = sub == 0

    for field in range(6):
        low, mid, high = low_ref[field], parent_ref[field], high_ref[field]
        if field % 3 == 2:
            wall = lax.broadcasted_iota(jnp.int32, mid.shape, 0) + place * rows > 0
            mid = jnp.where(wall, mid, 0.0)
        first[field, :TILE] = low
        first[field, TILE : TILE + rows] = mid
        first[field, TILE + rows :] = high
        second[field, :TILE] = low
        second[field, TILE + rows :] = high
    force[:TILE] = force_low_ref[...]
    force[TILE : TILE + rows] = force_ref[...]
    force[TILE + rows :] = force_high_ref[...]

    def at(block):
        return pl.ds(pl.multiple_of(block * TILE, TILE), TILE)

    def down(here, before):
        return jnp.where(bottom, pltpu.roll(before, 1, 0), pltpu.roll(here, 1, 0))

    def up(here, after):
        return jnp.where(top, pltpu.roll(after, TILE - 1, 0), pltpu.roll(here, TILE - 1, 0))

    def west(values):
        return pltpu.roll(values, 1, 1)

    def east(values):
        return pltpu.roll(values, columns - 1, 1)

    def heights(source, block):
        prev, here, after = at(jnp.maximum(block - 1, 0)), at(block), at(jnp.minimum(block + 1, blocks + 1))
        result = []
        for base in (0, 3):
            height = source[base, here]
            speed_u = source[base + 1, here]
            speed_v = source[base + 2, here]
            above_v = up(speed_v, source[base + 2, after])
            thick = 1.0 + height
            below_thick = 1.0 + down(height, source[base, prev])
            above_thick = 1.0 + up(height, source[base, after])
            flux_x = speed_u * (0.5 * (thick + west(thick)))
            flux_y = speed_v * (0.5 * (thick + below_thick))
            above_flux = above_v * (0.5 * (above_thick + thick))
            divergence = (east(flux_x) - flux_x) + (above_flux - flux_y)
            result.append((height - TIME_STEP * divergence, speed_u, speed_v, above_v))
        return result

    def block_step(source, target, shift, block, before):
        prev, here = at(jnp.maximum(block - 1, 0)), at(block)
        there = at(block - shift)
        parts = heights(source, block)
        row = (sub + ((block - 1) * TILE + place * rows)).astype(jnp.float32)
        coriolis_u = CORIOLIS_MEAN + (row * (1.0 / total) - 0.5)
        coriolis_v = CORIOLIS_MEAN + ((row - 0.5) * (1.0 / total) - 0.5)
        wall = row >= 1.0
        new = [part[0] for part in parts]
        ratios = (1.0, DENSITY_RATIO)
        for layer in range(2):
            base = 3 * layer
            _, speed_u, speed_v, above_v = parts[layer]
            if layer == 0:
                pressure = new[0] + new[1]
                below_pressure = before[0] + before[1]
                extra = force[here]
            else:
                pressure = DENSITY_RATIO * new[0] + new[1]
                below_pressure = DENSITY_RATIO * before[0] + before[1]
                extra = -DRAG_RATE * speed_u
            sum_v = speed_v + above_v
            mean_v = 0.25 * (sum_v + west(sum_v))
            new_u = speed_u + TIME_STEP * (coriolis_u * mean_v - (pressure - west(pressure)) + extra)
            sum_u = speed_u + down(speed_u, source[base + 1, prev])
            mean_u = 0.25 * (sum_u + east(sum_u))
            slope = pressure - down(pressure, below_pressure)
            new_v = speed_v + TIME_STEP * (-coriolis_v * mean_u - slope)
            target[base, there] = new[layer]
            target[base + 1, there] = new_u
            target[base + 2, there] = jnp.where(wall, new_v, 0.0)
        return tuple(new)

    start = jnp.where(place == 0, 1, 0)
    stop = jnp.where(place == count - 1, blocks + 1, blocks + 2)
    zero = jnp.zeros(tile, jnp.float32)
    source, target = first, second
    for _ in range(STEPS - 1):
        lax.fori_loop(start, stop, functools.partial(block_step, source, target, 0), (zero, zero))
        source, target = target, source
    edge = heights(source, 0)
    lax.fori_loop(1, blocks + 1, functools.partial(block_step, source, out_ref, 1), (edge[0][0], edge[1][0]))


def stencil(place, parents, low, high, forcing, force_low, force_high):
    fields_count, rows, columns = parents.shape
    grown = rows + 2 * TILE
    vmem = pl.BlockSpec(memory_space=pltpu.VMEM)
    return pl.pallas_call(
        functools.partial(stencil_kernel, lax.axis_size("lat")),
        out_shape=jax.ShapeDtypeStruct(parents.shape, jnp.float32),
        in_specs=[pl.BlockSpec(memory_space=pltpu.SMEM)] + [vmem] * 6,
        out_specs=vmem,
        scratch_shapes=[
            pltpu.VMEM((fields_count, grown, columns), jnp.float32),
            pltpu.VMEM((fields_count, grown, columns), jnp.float32),
            pltpu.VMEM((grown, columns), jnp.float32),
        ],
        cost_estimate=pl.CostEstimate(flops=300 * rows * columns, bytes_accessed=52 * rows * columns, transcendentals=0),
    )(place, parents, low, high, forcing, force_low, force_high)


def on_device(ensemble, forcing_table, ancestors, selector):
    forcing = lax.dynamic_index_in_dim(forcing_table, selector[0], 0, keepdims=False)
    force_low, force_high = edge_rows(forcing)
    parents = copy_members(ensemble, ancestors)
    low, high = edge_rows(parents)
    place = lax.axis_index("lat").astype(jnp.int32)[None]
    result = stencil(place, parents, low, high, forcing, force_low, force_high)
    return result.reshape(ensemble.shape)


def solution(mesh):
    placed = (
        P(("groups", "mem"), None, "lat", None),
        P(None, "lat", None),
        P("groups"),
        P(("groups", "mem")),
    )
    return jax.shard_map(
        on_device,
        mesh=mesh,
        in_specs=placed,
        out_specs=P(("groups", "mem"), None, "lat", None),
        check_vma=False,
    )
```

time: 565 us -> 107 us (0.19); the launches traced: 556 us -> 106 us
  other arithmetic: 307 us -> 1.3 us
  local copies, waits for them, and re-layouts: 150 us -> 4.83 us
  Pallas kernels: 0 us -> 14.9 us
  waiting for transfers between devices: 84.5 us -> 72.9 us
    unnamed x6 -> x0, other arithmetic: 292 us -> none
    unnamed x5 -> x4, local copies, waits for them, and re-layouts: 101 us -> 0.01 us
    all_to_all x2 -> x0, local copies, waits for them, and re-layouts: 20.5 us -> none  [the longest x1 18.4 us: copy_members(): lax.all_to_all(flat, 'mem', split_axis=2, concat_axis=0, tiled=True)]
    reshape x2 -> x0, local copies, waits for them, and re-layouts: 19.5 us -> none  [the longest x1 17.9 us: copy_members(): flat = block.reshape(slots, fields_count, band_rows * columns)]
    pallas_call x0 -> x1, Pallas kernels: none -> 14.9 us  [stencil(): pl.pallas_call(functools.partial(stencil_kernel, lax.axis_size('lat')), o...]
    all_to_all x2, waiting for transfers between devices: 82.6 us -> 72.2 us  [the longest x1 37.1 us: copy_members(): lax.all_to_all(pieces, 'mem', split_axis=0, concat_axis=0, tiled=True)]
    slice x79 -> x0, local copies, waits for them, and re-layouts: 6.49 us -> none  [the longest x36 2.71 us: col_east(): return jnp.roll(values, -1, axis=-1)]
  transfers between devices with their start and end apart: 4 -> 4, of which waited for: 3 -> 3; matrix products, arithmetic and copies ran while one was open for 0% -> 2% of each run, Pallas kernels for 0% -> 0%
where the time goes in v1:
time: 107 us; the launch traced here: 106 us
  waiting for transfers between devices  72.9 us (68%)
  Pallas kernels  14.9 us (14%)
  starting transfers between devices  11.8 us (11%)
  local copies, waits for them, and re-layouts  4.83 us (5%)
  other arithmetic  1.3 us (1%)
    all_to_all x1, waiting for transfers between devices, copy_members(): lax.all_to_all(pieces, 'mem', split_axis=0, concat_axis=0, tiled=True)  37.1 us
    all_to_all x1, waiting for transfers between devices, copy_members(): lax.all_to_all(taken, 'mem', split_axis=0, concat_axis=0, tiled=True)  35.1 us
    pallas_call x1, Pallas kernels, stencil(): pl.pallas_call(functools.partial(stencil_kernel, lax.axis_size('lat')), o...  14.9 us
    all_to_all x1, starting transfers between devices, copy_members(): lax.all_to_all(pieces, 'mem', split_axis=0, concat_axis=0, tiled=True)  7.41 us
    all_to_all x1, starting transfers between devices, copy_members(): lax.all_to_all(taken, 'mem', split_axis=0, concat_axis=0, tiled=True)  4.29 us
    gather x1, local copies, waits for them, and re-layouts, copy_members(): taken = jnp.take(spread, ancestors, axis=0, mode='clip')  3.2 us
  transfers between devices with their start and end apart: 4, of which 3 were waited for; matrix products, arithmetic and copies ran while one was open for 2% of the time, Pallas kernels for 0%

profile of v1, /device:TPU:0, one launch (start us, length us, event | category | flops | bytes accessed | tf_op | source)
XLA Modules:
  0.0 106.4 jit_solution(10620683931422752745)
XLA Ops:
  0.0 0.0 copy-start
  0.0 0.0 copy-start.1
  0.0 7.4 %all-to-all-start = ((f32[8,96,512]{2,1,0:T(8,128)}), f32[8,96,512]{2,1,0:T(8,128)}, u32[]{:S(2)}, u32[]{:S(2)}) async-start(f32[8,96,512]{2,1,0:T(8,128)} %bitcast.12), calls=%async_computation | async-start | bytes 3145728 | tf_op jit(solution)/shard_map/all_to_all | solution.py:25
  7.4 0.0 copy-done.1
  7.4 37.1 %all-to-all-done = f32[8,96,512]{2,1,0:T(8,128)} async-done(((f32[8,96,512]{2,1,0:T(8,128)}), f32[8,96,512]{2,1,0:T(8,128)}, u32[]{:S(2)}, u32[]{:S(2)}) %all-to-all-start) | async-done | bytes 1572896 | tf_op jit(solution)/shard_map/all_to_all | solution.py:25
  44.5 3.2 %gather_fusion = f32[8,96,512]{2,1,0:T(8,128)} fusion(f32[8,96,512]{2,1,0:T(8,128)} %all-to-all-done, s32[1024]{0:T(1024)S(1)} %pad_clamp_fusion), kind=kCustom, calls=%fused_computation | custom fusion | bytes 3145760 | tf_op jit(solution)/shard_map/jit(_take)/gather | solution.py:26
  47.7 4.3 %all-to-all-start.1 = ((f32[8,96,512]{2,1,0:T(8,128)}), f32[8,96,512]{2,1,0:T(8,128)}, u32[]{:S(2)}, u32[]{:S(2)}) async-start(f32[8,96,512]{2,1,0:T(8,128)} %gather_fusion), calls=%async_computation.1 | async-start | bytes 3145728 | tf_op jit(solution)/shard_map/all_to_all | solution.py:27
  52.7 0.0 copy-done
  52.7 0.1 collective-permute-start.1
  52.8 0.7 dynamic-slice_bitcast_fusion.force_ref
  53.5 35.1 %all-to-all-done.1 = f32[8,96,512]{2,1,0:T(8,128)} async-done(((f32[8,96,512]{2,1,0:T(8,128)}), f32[8,96,512]{2,1,0:T(8,128)}, u32[]{:S(2)}, u32[]{:S(2)}) %all-to-all-start.1) | async-done | bytes 1572896 | tf_op jit(solution)/shard_map/all_to_all | solution.py:27
  88.7 0.9 constant_dynamic-slice_fusion
  89.6 0.0 collective-permute-start
  89.6 0.0 collective-permute-done.1
  89.6 0.6 broadcast_select_fusion.2
  90.2 0.7 collective-permute-done
  90.9 0.7 broadcast_select_fusion
  91.6 14.9 %shard_map.46 = f32[6,128,512]{2,1,0:T(8,128)} custom-call(s32[1]{0:T(128)} %bitcast.place_ref, f32[6,128,512]{2,1,0:T(8,128)} %bitcast.2.parent_ref, f32[6,8,512]{2,1,0:T(8,128)} %get-tuple-element.6.low_ref, f32[6,8,512]{2,1,0:T(8,128)} %get-tuple-element.5.high_ref, f32[128,512]{1,0:T(8,128)} %dynamic-slice_bitcast_fusion.force_ref, ...), custom_call_target="tpu_custom_call" | custom-call | flops 19660800 | bytes 3407872 | tf_op jit(solution)/shard_map/pallas_call | solution.py:152
  (2 shorter events, 0.0 us)
Async XLA Ops:
  0.0 52.7 %copy-start = (f32[8,128,512]{2,1,0:T(8,128)S(1)}, f32[8,128,512]{2,1,0:T(8,128)}, u32[]{:S(2)}) copy-start(f32[8,128,512]{2,1,0:T(8,128)} %param.5) | copy-start | bytes 6291460
  0.0 7.4 %copy-start.1 = (s32[8]{0:T(128)S(1)}, s32[8]{0:T(128)}, u32[]{:S(2)}) copy-start(s32[8]{0:T(128)} %param.6) | copy-start | bytes 100
  0.0 44.5 %all-to-all-start = ((f32[8,96,512]{2,1,0:T(8,128)}), f32[8,96,512]{2,1,0:T(8,128)}, u32[]{:S(2)}, u32[]{:S(2)}) async-start(f32[8,96,512]{2,1,0:T(8,128)} %bitcast.12), calls=%async_computation | async-start | bytes 3145728 | tf_op jit(solution)/shard_map/all_to_all | solution.py:25
  47.7 40.9 %all-to-all-start.1 = ((f32[8,96,512]{2,1,0:T(8,128)}), f32[8,96,512]{2,1,0:T(8,128)}, u32[]{:S(2)}, u32[]{:S(2)}) async-start(f32[8,96,512]{2,1,0:T(8,128)} %gather_fusion), calls=%async_computation.1 | async-start | bytes 3145728 | tf_op jit(solution)/shard_map/all_to_all | solution.py:27
  52.7 36.9 %collective-permute-start.1 = (f32[8,512]{1,0:T(8,128)S(1)}, f32[8,512]{1,0:T(8,128)S(1)}, u32[]{:S(2)}, u32[]{:S(2)}) collective-permute-start(f32[8,512]{1,0:T(8,128)S(1)} %dynamic-slice_bitcast_fusion.1), channel_id=1, source_target_pairs={{0,1},{1,0},{2,3},{3,2},{4,5},{5,4},{6,7},{7,6},{8,9},{9,8},{10,11... | collective-permute-start | bytes 49160 | tf_op jit(solution)/shard_map/ppermute | solution.py:38
  89.6 1.3 %collective-permute-start = (f32[6,8,512]{2,1,0:T(8,128)S(1)}, f32[6,8,512]{2,1,0:T(8,128)S(1)}, u32[]{:S(2)}, u32[]{:S(2)}) collective-permute-start(f32[6,8,512]{2,1,0:T(8,128)S(1)} %constant_dynamic-slice_fusion), channel_id=1, source_target_pairs={{0,1},{1,0},{2,3},{3,2},{4,5},{5,4},{6,7},{7,6},{8,9},{9,8},{10,11... | collective-permute-start | bytes 294920 | tf_op jit(solution)/shard_map/ppermute | solution.py:38
